TPU v7x, 32 devices: a whole 2x2x4 slice. The times are simulated.
32 devices in a mesh: seq: 8 (over z, y), head: 4 (over x, core).
Axes of the slice: x: 2, y: 2, z: 4, core: 2. Of those that a mesh axis runs over, the one named last changes fastest.
Arguments:
- query: bfloat16 [4096, 1024], P('seq', 'head'), may hold values from -70 to 70
- key: bfloat16 [4096, 1024], P('seq', 'head'), may hold values from -15 to 15
- value: bfloat16 [4096, 1024], P('seq', 'head'), may hold values from -6 to 6
- middle_offsets: int32 [16], P('head'), may hold values from 0 to 3
- upper_offsets: int32 [16], P('head'), may hold values from 0 to 3
- out_weight: bfloat16 [1024, 1024], P('head'), may hold values from -0.1875 to 0.1875
Outputs:
- projected: bfloat16 [4096, 1024], P(('seq', 'head'))
All inputs are finite; a program needn't handle non-finite values.
Results may differ from a plain program's by a relative error of at most 0.0051.
Values may be sent and summed in bfloat16 or wider, within the bound.
A program may use at most 64 MiB of HBM per device.

v0:
```python
import jax
import jax.numpy as jnp
from jax import lax
from jax.sharding import PartitionSpec as P

HD = 64
SPAN = 8
MIDDLE_DILATION = 4


def partner_2(value, axis, stride):
    mask = 2**stride
    pairs = [(source, source ^ mask) for source in range(lax.axis_size(axis))]
    return lax.ppermute(value, axis, pairs)


def attend_segment(query_matrix_rows, key_matrix_rows, value_matrix_rows):
    scores = jnp.einsum(
        "qhd,khd->hqk", query_matrix_rows, key_matrix_rows, preferred_element_type=jnp.float32
    ) * HD ** (-0.5)
    row_max = jnp.max(scores, axis=2)
    mass = jnp.exp(scores - row_max[:, :, None])
    total = jnp.sum(mass, axis=2)
    soft_weights = mass.astype(jnp.bfloat16)
    weighted = jnp.einsum(
        "hqk,khd->qhd", soft_weights, value_matrix_rows, preferred_element_type=jnp.float32
    )
    return (weighted, total.T, row_max.T)


def attend_blocks(query_matrix_rows, key_matrix_rows, value_matrix_rows):
    block_size = min(512, query_matrix_rows.shape[0])
    pieces = query_matrix_rows.reshape(
        query_matrix_rows.shape[0] // block_size,
        block_size,
        query_matrix_rows.shape[1],
        query_matrix_rows.shape[2],
    )

    def one_block(one_piece):
        return attend_segment(one_piece, key_matrix_rows, value_matrix_rows)

    weighted, total, row_max = lax.map(one_block, pieces)
    return (
        weighted.reshape(query_matrix_rows.shape),
        total.reshape(query_matrix_rows.shape[:2]),
        row_max.reshape(query_matrix_rows.shape[:2]),
    )


def picked_rows(block_rows, offsets, stride):
    group_count = block_rows.shape[0] // stride
    grouped = block_rows.reshape(group_count, stride, block_rows.shape[1], block_rows.shape[2])
    chosen = (
        jnp.arange(stride, dtype=jnp.int32)[None, :, None, None] == offsets[None, None, :, None]
    )
    return jnp.sum(jnp.where(chosen, grouped, jnp.zeros((), grouped.dtype)), axis=1)


def scatter_rows(values, offsets, stride, filler):
    chosen = jnp.arange(stride, dtype=jnp.int32)[:, None] == offsets[None, :]
    spread_out = jnp.where(chosen[None], values[:, None], filler)
    return spread_out.reshape((values.shape[0] * stride,) + values.shape[1:])


def flatten_level(result):
    row_total = result[0].shape[0]
    weighted = result[0].reshape(row_total, -1)
    total = jnp.repeat(result[1], HD, axis=1)
    row_max = jnp.repeat(result[2], HD, axis=1)
    return (weighted, total, row_max)


def scatter_level(result, offsets, stride):
    weighted, total, row_max = flatten_level(result)
    column_offsets = jnp.repeat(offsets, HD)
    return (
        scatter_rows(weighted, column_offsets, stride, 0.0),
        scatter_rows(total, column_offsets, stride, 0.0),
        scatter_rows(row_max, column_offsets, stride, -jnp.inf),
    )


def combine(levels):
    highest = levels[0][2]
    for one_level in levels[1:]:
        highest = jnp.maximum(highest, one_level[2])
    numerator = jnp.zeros(levels[0][0].shape, jnp.float32)
    denominator = jnp.zeros(levels[0][1].shape, jnp.float32)
    for one_level in levels:
        factor = jnp.exp(one_level[2] - highest)
        numerator = numerator + factor * one_level[0]
        denominator = denominator + factor * one_level[1]
    return (numerator / denominator).astype(jnp.bfloat16)


def per_device(query, key, value, middle_offsets, upper_offsets, out_weight):
    row_count = query.shape[0]
    head_count = query.shape[1] // HD
    top_stride = lax.axis_size("seq") // 2
    query_matrix_rows = query.reshape(row_count, head_count, HD)
    key_matrix_rows = key.reshape(row_count, head_count, HD)
    value_matrix_rows = value.reshape(row_count, head_count, HD)
    top_key_local = picked_rows(key_matrix_rows, upper_offsets, top_stride).reshape(
        -1, head_count * HD
    )
    top_value_local = picked_rows(value_matrix_rows, upper_offsets, top_stride).reshape(
        -1, head_count * HD
    )
    top_key_all, top_value_all = (
        lax.all_gather(top_key_local, "seq", axis=0, tiled=True),
        lax.all_gather(top_value_local, "seq", axis=0, tiled=True),
    )
    upper_level = attend_segment(
        picked_rows(query_matrix_rows, upper_offsets, top_stride),
        top_key_all.reshape(-1, head_count, HD),
        top_value_all.reshape(-1, head_count, HD),
    )
    middle_pair = jnp.stack(
        [
            picked_rows(key_matrix_rows, middle_offsets, MIDDLE_DILATION),
            picked_rows(value_matrix_rows, middle_offsets, MIDDLE_DILATION),
        ]
    ).reshape(2, -1, head_count * HD)
    for bit_number in range(SPAN.bit_length() - 1):
        partner = partner_2(middle_pair, "seq", bit_number)
        middle_pair = jnp.concatenate([middle_pair, partner], axis=1)
    middle_level = attend_segment(
        picked_rows(query_matrix_rows, middle_offsets, MIDDLE_DILATION),
        middle_pair[0].reshape(-1, head_count, HD),
        middle_pair[1].reshape(-1, head_count, HD),
    )
    bottom = flatten_level(attend_blocks(query_matrix_rows, key_matrix_rows, value_matrix_rows))
    attention = combine(
        (
            bottom,
            scatter_level(middle_level, middle_offsets, MIDDLE_DILATION),
            scatter_level(upper_level, upper_offsets, top_stride),
        )
    )
    summed = lax.psum_scatter(
        jnp.dot(attention, out_weight, preferred_element_type=jnp.float32),
        "head",
        scatter_dimension=0,
        tiled=True,
    )
    return summed.astype(jnp.bfloat16)


def solution(mesh):
    in_specs = (
        P("seq", "head"),
        P("seq", "head"),
        P("seq", "head"),
        P("head"),
        P("head"),
        P("head", None),
    )
    out_specs = P(("seq", "head"), None)
    return jax.shard_map(
        per_device, mesh=mesh, in_specs=in_specs, out_specs=out_specs, check_vma=False
    )
```

profile of v0, /device:TPU:0, one launch (start us, length us, event | category | flops | bytes accessed | tf_op | source)
XLA Modules:
  0.0 164.0 jit_solution(4376389824751921904)
XLA Ops:
  6.5 1.3 reshape_reshape.16
  7.8 1.2 reshape_reshape.17
  9.1 1.3 reshape_reshape.18
  10.4 2.6 %select_reduce_fusion.4 = (bf16[128,4,64]{2,1,0:T(4,128)(2,1)S(1)}, bf16[128,4,64]{2,1,0:T(4,128)(2,1)S(1)}, bf16[128,4,64]{2,1,0:T(4,128)(2,1)S(1)}, bf16[128,4...) fusion(bf16[128,4,4,64]{3,2,1,0:T(4,128)(2,1)S(1)} %reshape_reshape.17, ...), kind=kLoop, calls=%fused_computation.41 | loop fusion | flops 1376256 | bytes 1179680 | tf_op jit(solution)/shard_map/reduce_sum | solution.py:57
  13.4 3.0 %collective-permute-start = (bf16[2,128,256]{1,2,0:T(8,128)(2,1)S(1)}, bf16[2,128,256]{1,2,0:T(8,128)(2,1)S(1)}, u32[]{:S(2)}, u32[]{:S(2)}) collective-permute-start(bf16[2,128,256]{1,2,0:T(8,128)(2,1)S(1)} %pad_maximum_fusion.3), channel_id=1, source_target_pairs={{0,4},{4,0},{8,12},{12,8},{16,20},{20,16},{24,28},{28,24},{1,5},{5... | collective-permute-start | bytes 393224 | tf_op jit(solution)/shard_map/ppermute | solution.py:14
  16.8 28.2 %all_gather.6 = bf16[1024,256]{0,1:T(8,128)(2,1)S(1)} all-gather(bf16[128,256]{0,1:T(8,128)(2,1)S(1)} %bitcast.102), channel_id=1, replica_groups=mesh['seq'=8,'head'=4] {'seq'}, dimensions={0}, use_global_device_ids=true | all-gather | bytes 589824 | tf_op jit(solution)/shard_map/all_gather | solution.py:111
  45.1 27.4 %all_gather.7 = bf16[1024,256]{0,1:T(8,128)(2,1)S(1)} all-gather(bf16[128,256]{0,1:T(8,128)(2,1)S(1)} %bitcast.103), channel_id=1, replica_groups=mesh['seq'=8,'head'=4] {'seq'}, dimensions={0}, use_global_device_ids=true | all-gather | bytes 589824 | tf_op jit(solution)/shard_map/all_gather | solution.py:112
  74.7 2.7 %multiply_reduce_fusion = (f32[4,512]{1,0:T(4,128)S(1)}, f32[4,512,512]{1,2,0:T(8,128)}) fusion(bf16[512,4,64]{0,2,1:T(8,128)(2,1)S(1)} %bitcast.94, bf16[512,4,64]{0,2,1:T(8,128)(2,1)S(1)} %bitcast.95), kind=kOutput, calls=%fused_computation.1 | convolution fusion | flops 136312832 | bytes 4726784 | tf_op jit(solution)/shard_map/while/body/eval_jaxpr/qhd,khd->hqk/dot_general | solution.py:18
  78.8 1.0 copy.73
  80.0 1.0 copy.82
  81.2 1.0 copy.86
  82.7 3.0 %fusion = f32[4,512]{1,0:T(4,128)S(1)} fusion(f32[4,512,512]{1,2,0:T(8,128)} %get-tuple-element.49, f32[4,512]{1,0:T(4,128)S(1)} %get-tuple-element.48), kind=kLoop, calls=%fused_computation.2 | loop fusion | flops 3143680 | bytes 4210688 | tf_op jit(solution)/shard_map/while/body/eval_jaxpr/reduce_sum | solution.py:23
  85.8 8.4 %collective-permute-done.1 = bf16[2,256,256]{1,2,0:T(8,128)(2,1)S(1)} collective-permute-done((bf16[2,256,256]{1,2,0:T(8,128)(2,1)S(1)}, bf16[2,256,256]{1,2,0:T(8,128)(2,1)S(1)}, u32[]{:S(2)}, u32[]{:S(2)}) %collective-permute-start.1) | collective-permute-done | bytes 262176 | tf_op jit(solution)/shard_map/ppermute | solution.py:14
  95.2 13.8 %collective-permute-done.2 = bf16[2,512,256]{1,2,0:T(8,128)(2,1)S(1)} collective-permute-done((bf16[2,512,256]{1,2,0:T(8,128)(2,1)S(1)}, bf16[2,512,256]{1,2,0:T(8,128)(2,1)S(1)}, u32[]{:S(2)}, u32[]{:S(2)}) %collective-permute-start.2) | collective-permute-done | bytes 524320 | tf_op jit(solution)/shard_map/ppermute | solution.py:14
  111.1 1.6 fusion.12
  112.9 1.4 broadcast_select_fusion.5
  114.7 2.2 %select_n.72 = f32[512,256]{1,0:T(8,128)} reshape(f32[128,4,256]{2,1,0:T(4,128)} %get-tuple-element.39) | data formatting | bytes 1048576 | tf_op jit(solution)/shard_map/jit(_where)/select_n | solution.py:62
  116.9 2.0 %copy.78 = f32[512,256]{0,1:T(8,128)} copy(f32[512,256]{1,0:T(8,128)} %select_n.72) | data formatting | bytes 1048576 | tf_op jit(solution)/shard_map/jit(_where)/select_n | solution.py:62
  118.9 2.0 %select_n.77 = f32[512,256]{1,0:T(8,128)} reshape(f32[128,4,256]{2,1,0:T(4,128)} %get-tuple-element.40) | data formatting | bytes 1048576 | tf_op jit(solution)/shard_map/jit(_where)/select_n | solution.py:62
  120.9 2.1 %copy.84 = f32[512,256]{0,1:T(8,128)} copy(f32[512,256]{1,0:T(8,128)} %select_n.77) | data formatting | bytes 1048576 | tf_op jit(solution)/shard_map/jit(_where)/select_n | solution.py:62
  123.0 1.6 fusion.28
  124.6 1.8 %fusion.37 = f32[512,1024]{1,0:T(8,128)} fusion(bf16[512,256]{0,1:T(8,128)(2,1)S(1)} %fusion.28, bf16[256,1024]{1,0:T(8,128)(2,1)S(1)} %copy-done), kind=kOutput, calls=%fused_computation.64 | convolution fusion | flops 268435456 | bytes 2883584 | tf_op jit(solution)/shard_map/dot_general | solution.py:142
  126.5 28.9 %reduce-scatter.2.cloned.1.call-done = f32[128,1024]{1,0:T(8,128)} async-done(((f32[512,1024]{1,0:T(8,128)}), f32[128,1024]{1,0:T(8,128)}) %reduce-scatter.2.cloned.1.call-update) | async-done | bytes 524304 | tf_op jit(solution)/shard_map/reduce_scatter | solution.py:141
  155.4 1.8 %convert_element_type.16 = bf16[128,1024]{1,0:T(8,128)(2,1)} convert(f32[128,1024]{1,0:T(8,128)} %reduce-scatter.2.cloned.1.call-done) | non-fusion elementwise | flops 131072 | bytes 786432 | tf_op jit(solution)/shard_map/convert_element_type | solution.py:147
  (66 shorter events, 8.8 us)
Async XLA Ops:
  6.5 118.1 %copy-start = (bf16[256,1024]{1,0:T(8,128)(2,1)S(1)}, bf16[256,1024]{1,0:T(8,128)(2,1)}, u32[]{:S(2)}) copy-start(bf16[256,1024]{1,0:T(8,128)(2,1)} %param.11) | copy-start | bytes 1572868
  6.5 3.9 %copy-start.8 = (s32[4]{0:T(128)S(1)}, s32[4]{0:T(128)}, u32[]{:S(2)}) copy-start(s32[4]{0:T(128)} %param.10) | copy-start | bytes 52
  6.5 3.9 %copy-start.9 = (s32[4]{0:T(128)S(1)}, s32[4]{0:T(128)}, u32[]{:S(2)}) copy-start(s32[4]{0:T(128)} %param.9) | copy-start | bytes 52
  6.5 148.9 %reduce-scatter.2.cloned.1.call-start = ((), (), s32[]{:S(2)}) async-start(), calls=%async_computation.1 | async-start | bytes 2621440 | tf_op jit(solution)/shard_map/reduce_scatter | solution.py:141
  9.1 7.3 %copy-start.5 = (bf16[512,256]{1,0:T(8,128)(2,1)S(1)}, bf16[512,256]{1,0:T(8,128)(2,1)}, u32[]{:S(2)}) copy-start(bf16[512,256]{1,0:T(8,128)(2,1)} %param.6) | copy-start | bytes 786436
  9.1 7.4 %copy-start.6 = (bf16[512,256]{1,0:T(8,128)(2,1)S(1)}, bf16[512,256]{1,0:T(8,128)(2,1)}, u32[]{:S(2)}) copy-start(bf16[512,256]{1,0:T(8,128)(2,1)} %param.7) | copy-start | bytes 786436
  13.4 68.8 %collective-permute-start = (bf16[2,128,256]{1,2,0:T(8,128)(2,1)S(1)}, bf16[2,128,256]{1,2,0:T(8,128)(2,1)S(1)}, u32[]{:S(2)}, u32[]{:S(2)}) collective-permute-start(bf16[2,128,256]{1,2,0:T(8,128)(2,1)S(1)} %pad_maximum_fusion.3), channel_id=1, source_target_pairs={{0,4},{4,0},{8,12},{12,8},{16,20},{20,16},{24,28},{28,24},{1,5},{5... | collective-permute-start | bytes 393224 | tf_op jit(solution)/shard_map/ppermute | solution.py:14
  77.4 0.9 copy-start.7
  82.2 12.0 %collective-permute-start.1 = (bf16[2,256,256]{1,2,0:T(8,128)(2,1)S(1)}, bf16[2,256,256]{1,2,0:T(8,128)(2,1)S(1)}, u32[]{:S(2)}, u32[]{:S(2)}) collective-permute-start(bf16[2,256,256]{1,2,0:T(8,128)(2,1)S(1)} %pad_maximum_fusion.2), channel_id=1, source_target_pairs={{0,8},{4,12},{8,0},{12,4},{16,24},{20,28},{24,16},{28,20},{1,9},{5... | collective-permute-start | bytes 786440 | tf_op jit(solution)/shard_map/ppermute | solution.py:14
  82.7 11.6 %copy-start.1 = (f32[4,512,512]{1,2,0:T(8,128)S(1)}, f32[4,512,512]{1,2,0:T(8,128)}, u32[]{:S(2)}) copy-start(f32[4,512,512]{1,2,0:T(8,128)} %get-tuple-element.49) | copy-start | bytes 12582916
  94.2 14.7 %collective-permute-start.2 = (bf16[2,512,256]{1,2,0:T(8,128)(2,1)S(1)}, bf16[2,512,256]{1,2,0:T(8,128)(2,1)S(1)}, u32[]{:S(2)}, u32[]{:S(2)}) collective-permute-start(bf16[2,512,256]{1,2,0:T(8,128)(2,1)S(1)} %pad_maximum_fusion.1), channel_id=1, source_target_pairs={{0,16},{4,20},{8,24},{12,28},{16,0},{20,4},{24,8},{28,12},{1,17},{... | collective-permute-start | bytes 1572872 | tf_op jit(solution)/shard_map/ppermute | solution.py:14
  114.7 8.3 %copy-start.2 = (f32[512,256]{0,1:T(8,128)S(1)}, f32[512,256]{0,1:T(8,128)}, u32[]{:S(2)}) copy-start(f32[512,256]{0,1:T(8,128)} %copy.73) | copy-start | bytes 1572868
  114.7 8.3 %copy-start.3 = (f32[512,256]{0,1:T(8,128)S(1)}, f32[512,256]{0,1:T(8,128)}, u32[]{:S(2)}) copy-start(f32[512,256]{0,1:T(8,128)} %copy.82) | copy-start | bytes 1572868
  114.7 8.3 %copy-start.4 = (f32[512,256]{0,1:T(8,128)S(1)}, f32[512,256]{0,1:T(8,128)}, u32[]{:S(2)}) copy-start(f32[512,256]{0,1:T(8,128)} %copy.86) | copy-start | bytes 1572868
Sparse Core Ops, SparseCore 0:
  126.6 28.7 reduce-scatter.1
where the time goes:
time: 165 us; the launch traced here: 164 us
  blocking collectives  55.6 us (34%)
  waiting for transfers between devices  51.2 us (31%)
  local copies, waits for them, and re-layouts  19.3 us (12%)
  between operations  13.7 us (8%)
  other arithmetic  12.1 us (7%)
  matrix products  8.54 us (5%)
  starting transfers between devices  3.61 us (2%)
    reduce_scatter x1, waiting for transfers between devices, per_device(): lax.psum_scatter(jnp.dot(attention, out_weight, preferred_element_type=jn...  28.9 us
    all_gather x1, blocking collectives, per_device(): lax.all_gather(top_key_local, 'seq', axis=0, tiled=True)  28.2 us
    all_gather x1, blocking collectives, per_device(): lax.all_gather(top_value_local, 'seq', axis=0, tiled=True)  27.4 us
    ppermute x3, waiting for transfers between devices, partner_2(): return lax.ppermute(value, axis, pairs)  22.2 us
    select_n x12, local copies, waits for them, and re-layouts, scatter_rows(): spread_out = jnp.where(chosen[None], values[:, None], filler)  12.2 us
    reduce_sum x3, other arithmetic, attend_segment(): total = jnp.sum(mass, axis=2)  4.04 us
    another operation x3, local copies, waits for them, and re-layouts, picked_rows(): block_rows.reshape(group_count, stride, block_rows.shape[1], block_rows.s...  3.82 us
    dot_general x3, matrix products, attend_segment(): jnp.einsum('qhd,khd->hqk', query_matrix_rows, key_matrix_rows, preferred_...  3.67 us
  transfers between devices with their start and end apart: 4, of which 3 were waited for; matrix products, arithmetic and copies ran while one was open for 8% of the time, Pallas kernels for 0%

commit v1 on v0

--- a/solution.py
+++ b/solution.py
@@ -6,6 +6,27 @@
 HD = 64
 SPAN = 8
 MIDDLE_DILATION = 4
+
+
+def gather_around(x, axis, dim):
+    devices, place, width = (lax.axis_size(axis), lax.axis_index(axis), x.shape[dim])
+    right = [(i, (i + 1) % devices) for i in range(devices)]
+    downward = [(i, (i - 1) % devices) for i in range(devices)]
+    result = jnp.zeros((*x.shape[:dim], devices * width, *x.shape[dim + 1 :]), x.dtype)
+    result = lax.dynamic_update_slice_in_dim(result, x, place * width, axis=dim)
+    from_left = from_right = x
+    middle = devices // 2
+    for hop in range(1, middle + 1):
+        from_left = lax.ppermute(from_left, axis, right)
+        result = lax.dynamic_update_slice_in_dim(
+            result, from_left, (place - hop) % devices * width, axis=dim
+        )
+        if hop < devices - middle:
+            from_right = lax.ppermute(from_right, axis, downward)
+            result = lax.dynamic_update_slice_in_dim(
+                result, from_right, (place + hop) % devices * width, axis=dim
+            )
+    return result
 
 
 def partner_2(value, axis, stride):
@@ -108,7 +129,7 @@
         -1, head_count * HD
     )
     top_key_all, top_value_all = (
-        lax.all_gather(top_key_local, "seq", axis=0, tiled=True),
+        gather_around(top_key_local, "seq", 0),
         lax.all_gather(top_value_local, "seq", axis=0, tiled=True),
     )
     upper_level = attend_segment(

time: 165 us -> 155 us (0.939)
  blocking collectives: 55.6 us -> 28.7 us
  starting transfers between devices: 3.61 us -> 15.7 us
  local copies, waits for them, and re-layouts: 19.3 us -> 23.4 us
  waiting for transfers between devices: 51.2 us -> 47.3 us
  other arithmetic: 12.1 us -> 15.8 us
    all_gather x1 -> x0, blocking collectives: 28.2 us -> none  [per_device(): lax.all_gather(top_key_local, 'seq', axis=0, tiled=True)]
    ppermute x3, waiting for transfers between devices: 22.2 us -> 5.3 us  [partner_2(): return lax.ppermute(value, axis, pairs)]
    ppermute x0 -> x7, starting transfers between devices: none -> 15.6 us  [the longest x3 12.1 us: gather_around(): from_right = lax.ppermute(from_right, axis, downward)]
    ppermute x0 -> x7, waiting for transfers between devices: none -> 11.9 us  [the longest x4 11.9 us: gather_around(): from_left = lax.ppermute(from_left, axis, right)]
    concatenate x3, other arithmetic: 0.21 us -> 3.74 us  [per_device(): middle_pair = jnp.concatenate([middle_pair, partner], axis=1)]
    ppermute x3, starting transfers between devices: 3.6 us -> 0.08 us  [partner_2(): return lax.ppermute(value, axis, pairs)]
    broadcast_in_dim x6, local copies, waits for them, and re-layouts: 0.57 us -> 3.03 us  [scatter_rows(): spread_out = jnp.where(chosen[None], values[:, None], filler)]
    reduce_sum x3, other arithmetic: 4.04 us -> 1.67 us  [attend_segment(): total = jnp.sum(mass, axis=2)]
  transfers between devices with their start and end apart: 4 -> 11, of which waited for: 3 -> 5; matrix products, arithmetic and copies ran while one was open for 8% -> 12% of each run, Pallas kernels for 0% -> 0%
where the time goes in v1:
time: 155 us; the launch traced here: 154 us
  waiting for transfers between devices  47.3 us (31%)
  blocking collectives  28.7 us (19%)
  local copies, waits for them, and re-layouts  23.4 us (15%)
  other arithmetic  15.8 us (10%)
  starting transfers between devices  15.7 us (10%)
  between operations  14 us (9%)
  matrix products  9.22 us (6%)
    reduce_scatter x1, waiting for transfers between devices, per_device(): lax.psum_scatter(jnp.dot(attention, out_weight, preferred_element_type=jn...  30.1 us
    all_gather x1, blocking collectives, per_device(): lax.all_gather(top_value_local, 'seq', axis=0, tiled=True)  28.7 us
    select_n x12, local copies, waits for them, and re-layouts, scatter_rows(): spread_out = jnp.where(chosen[None], values[:, None], filler)  12.2 us
    ppermute x3, starting transfers between devices, gather_around(): from_right = lax.ppermute(from_right, axis, downward)  12.1 us
    ppermute x4, waiting for transfers between devices, gather_around(): from_left = lax.ppermute(from_left, axis, right)  11.9 us
    ppermute x3, waiting for transfers between devices, partner_2(): return lax.ppermute(value, axis, pairs)  5.3 us
    dot_general x3, matrix products, attend_segment(): jnp.einsum('hqk,khd->qhd', soft_weights, value_matrix_rows, preferred_ele...  4.73 us
    another operation x3, local copies, waits for them, and re-layouts, picked_rows(): block_rows.reshape(group_count, stride, block_rows.shape[1], block_rows.s...  3.81 us
  transfers between devices with their start and end apart: 11, of which 5 were waited for; matrix products, arithmetic and copies ran while one was open for 12% of the time, Pallas kernels for 0%

profile of v1, /device:TPU:0, one launch (start us, length us, event | category | flops | bytes accessed | tf_op | source)
XLA Modules:
  0.0 154.2 jit_solution(723842470958949234)
XLA Ops:
  10.4 3.3 %select_reduce_fusion.4 = (bf16[128,4,64]{2,1,0:T(4,128)(2,1)S(1)}, bf16[128,4,64]{2,1,0:T(4,128)(2,1)S(1)}, bf16[128,4,64]{2,1,0:T(4,128)(2,1)S(1)}, bf16[128,4...) fusion(bf16[128,4,4,64]{3,2,1,0:T(4,128)(2,1)S(1)} %reshape_reshape.17, ...), kind=kLoop, calls=%fused_computation.41 | loop fusion | flops 1376256 | bytes 1179680 | tf_op jit(solution)/shard_map/reduce_sum | solution.py:78
  13.8 3.0 %collective-permute-start.3 = (bf16[128,256]{0,1:T(8,128)(2,1)S(1)}, bf16[128,256]{0,1:T(8,128)(2,1)S(1)}, u32[]{:S(2)}, u32[]{:S(2)}) collective-permute-start(bf16[128,256]{0,1:T(8,128)(2,1)S(1)} %bitcast.103), channel_id=1, source_target_pairs={{0,4},{4,8},{8,12},{12,16},{16,20},{20,24},{24,28},{28,0},{1,5},{5... | collective-permute-start | bytes 196616 | tf_op jit(solution)/shard_map/ppermute | solution.py:20
  16.8 3.1 %collective-permute-start.4 = (bf16[128,256]{0,1:T(8,128)(2,1)S(1)}, bf16[128,256]{0,1:T(8,128)(2,1)S(1)}, u32[]{:S(2)}, u32[]{:S(2)}) collective-permute-start(bf16[128,256]{0,1:T(8,128)(2,1)S(1)} %bitcast.104), channel_id=1, source_target_pairs={{0,28},{4,0},{8,4},{12,8},{16,12},{20,16},{24,20},{28,24},{1,29},{... | collective-permute-start | bytes 196616 | tf_op jit(solution)/shard_map/ppermute | solution.py:25
  21.7 28.7 %all_gather.3 = bf16[1024,256]{0,1:T(8,128)(2,1)} all-gather(bf16[128,256]{0,1:T(8,128)(2,1)S(1)} %bitcast.102), channel_id=1, replica_groups=mesh['seq'=8,'head'=4] {'seq'}, dimensions={0}, use_global_device_ids=true | all-gather | bytes 589824 | tf_op jit(solution)/shard_map/all_gather | solution.py:133
  54.2 4.3 %collective-permute-start.6 = (bf16[128,256]{0,1:T(8,128)(2,1)S(1)}, bf16[128,256]{0,1:T(8,128)(2,1)S(1)}, u32[]{:S(2)}, u32[]{:S(2)}) collective-permute-start(bf16[128,256]{0,1:T(8,128)(2,1)S(1)} %collective-permute-done.4), channel_id=1, source_target_pairs={{0,28},{4,0},{8,4},{12,8},{16,12},{20,16},{24,20},{28,24},{1,29},{... | collective-permute-start | bytes 196616 | tf_op jit(solution)/shard_map/ppermute | solution.py:25
  59.3 2.2 %collective-permute-done.5 = bf16[128,256]{0,1:T(8,128)(2,1)S(1)} collective-permute-done((bf16[128,256]{0,1:T(8,128)(2,1)S(1)}, bf16[128,256]{0,1:T(8,128)(2,1)S(1)}, u32[]{:S(2)}, u32[]{:S(2)}) %collective-permute-start.5) | collective-permute-done | bytes 65568 | tf_op jit(solution)/shard_map/ppermute | solution.py:20
  61.5 4.7 %collective-permute-start.8 = (bf16[128,256]{0,1:T(8,128)(2,1)S(1)}, bf16[128,256]{0,1:T(8,128)(2,1)S(1)}, u32[]{:S(2)}, u32[]{:S(2)}) collective-permute-start(bf16[128,256]{0,1:T(8,128)(2,1)S(1)} %collective-permute-done.6), channel_id=1, source_target_pairs={{0,28},{4,0},{8,4},{12,8},{16,12},{20,16},{24,20},{28,24},{1,29},{... | collective-permute-start | bytes 196616 | tf_op jit(solution)/shard_map/ppermute | solution.py:25
  66.2 2.2 %collective-permute-done.7 = bf16[128,256]{0,1:T(8,128)(2,1)S(1)} collective-permute-done((bf16[128,256]{0,1:T(8,128)(2,1)S(1)}, bf16[128,256]{0,1:T(8,128)(2,1)S(1)}, u32[]{:S(2)}, u32[]{:S(2)}) %collective-permute-start.7) | collective-permute-done | bytes 65568 | tf_op jit(solution)/shard_map/ppermute | solution.py:20
  68.5 7.5 %collective-permute-done.9 = bf16[128,256]{0,1:T(8,128)(2,1)S(1)} collective-permute-done((bf16[128,256]{0,1:T(8,128)(2,1)S(1)}, bf16[128,256]{0,1:T(8,128)(2,1)S(1)}, u32[]{:S(2)}, u32[]{:S(2)}) %collective-permute-start.9) | collective-permute-done | bytes 65568 | tf_op jit(solution)/shard_map/ppermute | solution.py:20
  76.0 1.4 multiply_reduce_fusion.1
  79.2 1.7 %copy.92 = f32[128,256]{1,0:T(8,128)} copy(f32[128,256]{0,1:T(8,128)} %bitcast.98) | data formatting | bytes 262144 | tf_op jit(solution)/shard_map/jit(_where)/broadcast_in_dim | solution.py:83
  80.8 1.8 %pad_maximum_fusion.1 = bf16[2,512,256]{1,2,0:T(8,128)(2,1)} fusion(bf16[2,256,256]{1,2,0:T(8,128)(2,1)} %collective-permute-done.1, bf16[2,128,256]{1,2,0:T(8,128)(2,1)S(1)} %collective-permute-done, bf16[1,128,256]{1,2,0:T(8,128)(2,1)S(1)} %bitcast.91, bf16[1,128,256]{1,2,0:T(8,128)(2,1)S(1)} %bitcast.87), kind=kLoop, calls=%fused_computation.26 | loop fusion | flops 2097152 | bytes 1048576 | tf_op jit(solution)/shard_map/concatenate | solution.py:148
  82.6 2.3 %fusion.10 = f32[4,64,128]{2,1,0:T(8,128)} fusion(bf16[1024,4,64]{0,2,1:T(8,128)(2,1)} %bitcast.81, f32[4,128,1024]{2,1,0:T(8,128)S(1)} %get-tuple-element.45, f32[4,128]{1,0:T(4,128)} %copy-done.8), kind=kOutput, calls=%fused_computation.15 | convolution fusion | flops 68681728 | bytes 2754560 | tf_op jit(solution)/shard_map/hqk,khd->qhd/dot_general | solution.py:46
  91.5 5.3 %collective-permute-done.2 = bf16[2,512,256]{1,2,0:T(8,128)(2,1)} collective-permute-done((bf16[2,512,256]{1,2,0:T(8,128)(2,1)}, bf16[2,512,256]{1,2,0:T(8,128)(2,1)}, u32[]{:S(2)}, u32[]{:S(2)}) %collective-permute-start.2) | collective-permute-done | bytes 524320 | tf_op jit(solution)/shard_map/ppermute | solution.py:35
  100.1 1.6 %fusion.12 = f32[4,64,128]{2,1,0:T(8,128)S(1)} fusion(bf16[1024,4,64]{0,2,1:T(8,128)(2,1)} %bitcast.83, f32[4,128,1024]{2,1,0:T(8,128)S(1)} %get-tuple-element.47, f32[4,128]{1,0:T(4,128)} %copy-done.9), kind=kOutput, calls=%fused_computation.16 | convolution fusion | flops 68681728 | bytes 2754560 | tf_op jit(solution)/shard_map/hqk,khd->qhd/dot_general | solution.py:46
  102.0 1.3 broadcast_select_fusion.5
  103.7 2.1 %select_n.142 = f32[512,256]{1,0:T(8,128)} reshape(f32[128,4,256]{2,1,0:T(4,128)} %get-tuple-element.39) | data formatting | bytes 1048576 | tf_op jit(solution)/shard_map/jit(_where)/select_n | solution.py:83
  105.9 2.1 %copy.85 = f32[512,256]{0,1:T(8,128)} copy(f32[512,256]{1,0:T(8,128)} %select_n.142) | data formatting | bytes 1048576 | tf_op jit(solution)/shard_map/jit(_where)/select_n | solution.py:83
  107.9 2.0 %select_n.147 = f32[512,256]{1,0:T(8,128)} reshape(f32[128,4,256]{2,1,0:T(4,128)} %get-tuple-element.40) | data formatting | bytes 1048576 | tf_op jit(solution)/shard_map/jit(_where)/select_n | solution.py:83
  109.9 2.0 %copy.91 = f32[512,256]{0,1:T(8,128)} copy(f32[512,256]{1,0:T(8,128)} %select_n.147) | data formatting | bytes 1048576 | tf_op jit(solution)/shard_map/jit(_where)/select_n | solution.py:83
  112.0 1.6 %fusion.28 = bf16[512,256]{0,1:T(8,128)(2,1)S(1)} fusion(f32[512,256]{0,1:T(8,128)S(1)} %copy-done.3, f32[512,256]{0,1:T(8,128)} %copy.91, f32[512,256]{0,1:T(8,128)S(1)} %copy-done.2, f32[512,256]{0,1:T(8,128)S(1)} %copy-done.1, f32[512,256]{0,1:T(8,128)} %copy.85, f32[512,256]{0,1:T(8,128)S(1)} %copy.76, f32[4,512,64]{1,2,0:T(8,128)S(1)} %fusion.2, ...), kind=kLoop, calls=%fused_computation.43 | loop fusion | flops 2228224 | bytes 3948544 | tf_op jit(solution)/shard_map/convert_element_type | solution.py:115
  113.6 1.8 %fusion.37 = f32[512,1024]{1,0:T(8,128)} fusion(bf16[512,256]{0,1:T(8,128)(2,1)S(1)} %fusion.28, bf16[256,1024]{1,0:T(8,128)(2,1)S(1)} %copy-done), kind=kOutput, calls=%fused_computation.72 | convolution fusion | flops 268435456 | bytes 2883584 | tf_op jit(solution)/shard_map/dot_general | solution.py:163
  115.5 30.1 %reduce-scatter.2.cloned.1.call-done = f32[128,1024]{1,0:T(8,128)} async-done(((f32[512,1024]{1,0:T(8,128)}), f32[128,1024]{1,0:T(8,128)}) %reduce-scatter.2.cloned.1.call-update) | async-done | bytes 524304 | tf_op jit(solution)/shard_map/reduce_scatter | solution.py:162
  145.6 1.8 %convert_element_type.16 = bf16[128,1024]{1,0:T(8,128)(2,1)} convert(f32[128,1024]{1,0:T(8,128)} %reduce-scatter.2.cloned.1.call-done) | non-fusion elementwise | flops 131072 | bytes 786432 | tf_op jit(solution)/shard_map/convert_element_type | solution.py:168
  (96 shorter events, 22.3 us)
Async XLA Ops:
  6.5 107.1 %copy-start = (bf16[256,1024]{1,0:T(8,128)(2,1)S(1)}, bf16[256,1024]{1,0:T(8,128)(2,1)}, u32[]{:S(2)}) copy-start(bf16[256,1024]{1,0:T(8,128)(2,1)} %param.11) | copy-start | bytes 1572868
  6.5 3.8 %copy-start.13 = (s32[4]{0:T(128)S(1)}, s32[4]{0:T(128)}, u32[]{:S(2)}) copy-start(s32[4]{0:T(128)} %param.10) | copy-start | bytes 52
  6.5 3.9 %copy-start.12 = (s32[4]{0:T(128)S(1)}, s32[4]{0:T(128)}, u32[]{:S(2)}) copy-start(s32[4]{0:T(128)} %param.9) | copy-start | bytes 52
  6.5 139.1 %reduce-scatter.2.cloned.1.call-start = ((), (), s32[]{:S(2)}) async-start(), calls=%async_computation.1 | async-start | bytes 2621440 | tf_op jit(solution)/shard_map/reduce_scatter | solution.py:162
  9.1 11.3 %copy-start.4 = (bf16[512,256]{1,0:T(8,128)(2,1)S(1)}, bf16[512,256]{1,0:T(8,128)(2,1)}, u32[]{:S(2)}) copy-start(bf16[512,256]{1,0:T(8,128)(2,1)} %param.6) | copy-start | bytes 786436
  10.4 10.2 %copy-start.5 = (bf16[512,256]{1,0:T(8,128)(2,1)S(1)}, bf16[512,256]{1,0:T(8,128)(2,1)}, u32[]{:S(2)}) copy-start(bf16[512,256]{1,0:T(8,128)(2,1)} %param.7) | copy-start | bytes 786436
  10.4 10.3 %copy-start.6 = (bf16[512,256]{1,0:T(8,128)(2,1)S(1)}, bf16[512,256]{1,0:T(8,128)(2,1)}, u32[]{:S(2)}) copy-start(bf16[512,256]{1,0:T(8,128)(2,1)} %param.8) | copy-start | bytes 786436
  13.7 7.9 %copy-start.7 = (bf16[128,4,64]{2,1,0:T(4,128)(2,1)S(1)}, bf16[128,4,64]{2,1,0:T(4,128)(2,1)}, u32[]{:S(2)}) copy-start(bf16[128,4,64]{2,1,0:T(4,128)(2,1)} %get-tuple-element.33) | copy-start | bytes 196612
  13.8 39.9 %collective-permute-start.3 = (bf16[128,256]{0,1:T(8,128)(2,1)S(1)}, bf16[128,256]{0,1:T(8,128)(2,1)S(1)}, u32[]{:S(2)}, u32[]{:S(2)}) collective-permute-start(bf16[128,256]{0,1:T(8,128)(2,1)S(1)} %bitcast.103), channel_id=1, source_target_pairs={{0,4},{4,8},{8,12},{12,16},{16,20},{20,24},{24,28},{28,0},{1,5},{5... | collective-permute-start | bytes 196616 | tf_op jit(solution)/shard_map/ppermute | solution.py:20
  16.8 37.4 %collective-permute-start.4 = (bf16[128,256]{0,1:T(8,128)(2,1)S(1)}, bf16[128,256]{0,1:T(8,128)(2,1)S(1)}, u32[]{:S(2)}, u32[]{:S(2)}) collective-permute-start(bf16[128,256]{0,1:T(8,128)(2,1)S(1)} %bitcast.104), channel_id=1, source_target_pairs={{0,28},{4,0},{8,4},{12,8},{16,12},{20,16},{24,20},{28,24},{1,29},{... | collective-permute-start | bytes 196616 | tf_op jit(solution)/shard_map/ppermute | solution.py:25
  20.2 38.3 %collective-permute-start = (bf16[2,128,256]{1,2,0:T(8,128)(2,1)S(1)}, bf16[2,128,256]{1,2,0:T(8,128)(2,1)S(1)}, u32[]{:S(2)}, u32[]{:S(2)}) collective-permute-start(bf16[2,128,256]{1,2,0:T(8,128)(2,1)S(1)} %pad_maximum_fusion.3), channel_id=1, source_target_pairs={{0,4},{4,0},{8,12},{12,8},{16,20},{20,16},{24,28},{28,24},{1,5},{5... | collective-permute-start | bytes 393224 | tf_op jit(solution)/shard_map/ppermute | solution.py:35
  53.7 7.8 %collective-permute-start.5 = (bf16[128,256]{0,1:T(8,128)(2,1)S(1)}, bf16[128,256]{0,1:T(8,128)(2,1)S(1)}, u32[]{:S(2)}, u32[]{:S(2)}) collective-permute-start(bf16[128,256]{0,1:T(8,128)(2,1)S(1)} %collective-permute-done.3), channel_id=1, source_target_pairs={{0,4},{4,8},{8,12},{12,16},{16,20},{20,24},{24,28},{28,0},{1,5},{5... | collective-permute-start | bytes 196616 | tf_op jit(solution)/shard_map/ppermute | solution.py:20
  54.2 7.3 %collective-permute-start.6 = (bf16[128,256]{0,1:T(8,128)(2,1)S(1)}, bf16[128,256]{0,1:T(8,128)(2,1)S(1)}, u32[]{:S(2)}, u32[]{:S(2)}) collective-permute-start(bf16[128,256]{0,1:T(8,128)(2,1)S(1)} %collective-permute-done.4), channel_id=1, source_target_pairs={{0,28},{4,0},{8,4},{12,8},{16,12},{20,16},{24,20},{28,24},{1,29},{... | collective-permute-start | bytes 196616 | tf_op jit(solution)/shard_map/ppermute | solution.py:25
  59.3 21.6 %collective-permute-start.1 = (bf16[2,256,256]{1,2,0:T(8,128)(2,1)}, bf16[2,256,256]{1,2,0:T(8,128)(2,1)}, u32[]{:S(2)}, u32[]{:S(2)}) collective-permute-start(bf16[2,256,256]{1,2,0:T(8,128)(2,1)} %pad_maximum_fusion.2), channel_id=1, source_target_pairs={{0,8},{4,12},{8,0},{12,4},{16,24},{20,28},{24,16},{28,20},{1,9},{5... | collective-permute-start | bytes 786440 | tf_op jit(solution)/shard_map/ppermute | solution.py:35
  61.5 7.0 %collective-permute-start.7 = (bf16[128,256]{0,1:T(8,128)(2,1)S(1)}, bf16[128,256]{0,1:T(8,128)(2,1)S(1)}, u32[]{:S(2)}, u32[]{:S(2)}) collective-permute-start(bf16[128,256]{0,1:T(8,128)(2,1)S(1)} %collective-permute-done.5), channel_id=1, source_target_pairs={{0,4},{4,8},{8,12},{12,16},{16,20},{20,24},{24,28},{28,0},{1,5},{5... | collective-permute-start | bytes 196616 | tf_op jit(solution)/shard_map/ppermute | solution.py:20
  61.5 7.0 %collective-permute-start.8 = (bf16[128,256]{0,1:T(8,128)(2,1)S(1)}, bf16[128,256]{0,1:T(8,128)(2,1)S(1)}, u32[]{:S(2)}, u32[]{:S(2)}) collective-permute-start(bf16[128,256]{0,1:T(8,128)(2,1)S(1)} %collective-permute-done.6), channel_id=1, source_target_pairs={{0,28},{4,0},{8,4},{12,8},{16,12},{20,16},{24,20},{28,24},{1,29},{... | collective-permute-start | bytes 196616 | tf_op jit(solution)/shard_map/ppermute | solution.py:25
  68.4 7.6 %collective-permute-start.9 = (bf16[128,256]{0,1:T(8,128)(2,1)S(1)}, bf16[128,256]{0,1:T(8,128)(2,1)S(1)}, u32[]{:S(2)}, u32[]{:S(2)}) collective-permute-start(bf16[128,256]{0,1:T(8,128)(2,1)S(1)} %collective-permute-done.7), channel_id=1, source_target_pairs={{0,4},{4,8},{8,12},{12,16},{16,20},{20,24},{24,28},{28,0},{1,5},{5... | collective-permute-start | bytes 196616 | tf_op jit(solution)/shard_map/ppermute | solution.py:20
  77.4 0.6 copy-start.8
  82.6 14.2 %collective-permute-start.2 = (bf16[2,512,256]{1,2,0:T(8,128)(2,1)}, bf16[2,512,256]{1,2,0:T(8,128)(2,1)}, u32[]{:S(2)}, u32[]{:S(2)}) collective-permute-start(bf16[2,512,256]{1,2,0:T(8,128)(2,1)} %pad_maximum_fusion.1), channel_id=1, source_target_pairs={{0,16},{4,20},{8,24},{12,28},{16,0},{20,4},{24,8},{28,12},{1,17},{... | collective-permute-start | bytes 1572872 | tf_op jit(solution)/shard_map/ppermute | solution.py:35
  99.9 2.1 %copy-start.11 = (pred[4,256]{1,0:T(4,128)(4,1)S(1)}, pred[4,256]{1,0:T(4,128)(4,1)}, u32[]{:S(2)}) copy-start(pred[4,256]{1,0:T(4,128)(4,1)} %iota_compare_fusion.1) | copy-start | bytes 3076
  100.0 1.8 %copy-start.10 = (f32[4,128]{1,0:T(4,128)S(1)}, f32[4,128]{1,0:T(4,128)}, u32[]{:S(2)}) copy-start(f32[4,128]{1,0:T(4,128)} %copy-done.9) | copy-start | bytes 6148
  103.7 8.3 %copy-start.1 = (f32[512,256]{0,1:T(8,128)S(1)}, f32[512,256]{0,1:T(8,128)}, u32[]{:S(2)}) copy-start(f32[512,256]{0,1:T(8,128)} %copy.80) | copy-start | bytes 1572868
  103.7 8.3 %copy-start.2 = (f32[512,256]{0,1:T(8,128)S(1)}, f32[512,256]{0,1:T(8,128)}, u32[]{:S(2)}) copy-start(f32[512,256]{0,1:T(8,128)} %copy.89) | copy-start | bytes 1572868
  103.7 8.3 %copy-start.3 = (f32[512,256]{0,1:T(8,128)S(1)}, f32[512,256]{0,1:T(8,128)}, u32[]{:S(2)}) copy-start(f32[512,256]{0,1:T(8,128)} %copy.93) | copy-start | bytes 1572868
  (1 other events, 0.6 us)
Sparse Core Ops, SparseCore 0:
  115.6 29.9 reduce-scatter.1
